TPU v7x, 32 devices: a whole 2x2x4 slice. The times are simulated.
32 devices in a mesh: seg: 2 (over y), chan: 8 (over z, x), band: 2 (over core).
Axes of the slice: x: 2, y: 2, z: 4, core: 2. Of those that a mesh axis runs over, the one named last changes fastest.
Arguments:
- strain: float32 [2048, 8, 3000], P(('seg', 'chan'), 'band'), parts along dimension 0, may hold values from -84 to 84
- offsets: int32 [16, 6], P(('seg', 'band')), parts along dimension 0, may hold values from 0 to 2000, as said below
- bins: int32 [256], replicated, may hold values from 1 to 499, as said below
Outputs:
- cross_spectra: bfloat16 [2048, 1024, 2, 256], P(('seg', 'chan'), None, None, 'band'), parts along dimension 0
There are 2 independent parts, one for each index of `seg`. A program takes and returns all parts, laid end to end along the dimension named above; an argument that names none is the same for every part. Nothing has to cross between parts.
Inputs may be any that keep to these rules, and one draw needn't show every extreme that they name: `offsets`: each window lies inside its minute file. `bins`: ascending and distinct.
All inputs are finite; a program needn't handle non-finite values.
Results may differ from a plain program's by a relative error of at most 0.0062.
Values may be sent and summed in bfloat16 or wider, within the bound.
A program may use at most 320 MiB of HBM per device.

v0:
```python
import math

import jax
import jax.numpy as jnp
from jax import lax
from jax.sharding import PartitionSpec as P

WIN_LEN = 1000
GROUP = 128
REACH = 64


def normalize(strain):
    width = 2 * REACH + 1
    magnitude = jnp.abs(strain)
    zero_val = jnp.zeros((), magnitude.dtype)
    running = lax.reduce_window(
        magnitude, zero_val, lax.add, (1, 1, width), (1, 1, 1), ((0, 0), (0, 0), (REACH, REACH))
    )
    unit_row = jnp.ones((strain.shape[2],), magnitude.dtype)
    counts = lax.reduce_window(unit_row, zero_val, lax.add, (width,), (1,), ((REACH, REACH),))
    return strain / (running / counts + 1e-06)


def cut_windows(normed, offsets):

    def one_file(rows, starts):
        return jax.vmap(lambda start_pos: lax.dynamic_slice_in_dim(rows, start_pos, WIN_LEN, 1))(
            starts
        )

    pieces = jax.vmap(one_file, in_axes=(1, 0))(normed, offsets)
    sample_pos = jnp.arange(WIN_LEN, dtype=jnp.float32)
    hann_taper = 0.5 - 0.5 * jnp.cos(2.0 * math.pi * (sample_pos + 0.5) / WIN_LEN)
    return (jnp.transpose(pieces, (2, 0, 1, 3)) * hann_taper).astype(jnp.bfloat16)


def make_table(bins):
    sample_idx = jnp.arange(WIN_LEN, dtype=jnp.int32)
    phase_idx = sample_idx[:, None] * bins[None, :] % WIN_LEN
    angles = phase_idx.astype(jnp.float32) * (2.0 * math.pi / WIN_LEN)
    return jnp.concatenate([jnp.cos(angles), -jnp.sin(angles)], axis=1).astype(jnp.bfloat16)


def spectra(windows, table):
    flat_rows = windows.reshape(-1, WIN_LEN)
    result = jnp.dot(flat_rows, table, preferred_element_type=jnp.float32)
    return result.reshape(
        windows.shape[0], windows.shape[1] * windows.shape[2], 2, table.shape[1] // 2
    )


def whiten(spec):
    chan_rows, win_count, _, bin_count = spec.shape
    grouped = spec.reshape(chan_rows, win_count, 2, bin_count // GROUP, GROUP)
    power_mean = jnp.mean(jnp.sum(grouped * grouped, axis=2), axis=-1, keepdims=True)
    gain_inv = lax.rsqrt(power_mean + 1e-06)[:, :, None]
    return (grouped * gain_inv).reshape(spec.shape).astype(jnp.bfloat16)


def cross_block(lhs_rows, other, win_count):
    products = jnp.einsum("iwcf,jwcf->ijf", lhs_rows, other, preferred_element_type=jnp.float32)
    chan_rows = lhs_rows.shape[0] // 2
    split_parts = products.reshape(2, chan_rows, other.shape[0], products.shape[2])
    return (jnp.transpose(split_parts, (1, 2, 0, 3)) / win_count).astype(jnp.bfloat16)


def on_device(strain, offsets, bins):
    normed = normalize(strain)
    windows = cut_windows(normed, offsets)
    band_count = lax.axis_size("band")
    bin_share = bins.shape[0] // band_count
    all_windows = lax.all_gather(windows, "band", axis=1, tiled=True)
    my_bins = lax.dynamic_slice_in_dim(bins, lax.axis_index("band") * bin_share, bin_share)
    whitened = whiten(spectra(all_windows, make_table(my_bins)))
    chan_rows = whitened.shape[0]
    win_count = whitened.shape[1]
    rotated = jnp.stack([whitened[:, :, 1], -whitened[:, :, 0]], axis=2)
    lhs_rows = jnp.concatenate([whitened, rotated], axis=0)
    chan_count = lax.axis_size("chan")
    col_count = chan_rows * chan_count
    blank_out = jnp.zeros((chan_rows, col_count, 2, bin_share), jnp.bfloat16)
    return lax.dynamic_update_slice_in_dim(
        blank_out,
        cross_block(lhs_rows, lax.all_gather(whitened, "chan", axis=0, tiled=True), win_count),
        jnp.int32(0),
        1,
    )


def solution(mesh):
    placed = (P(("seg", "chan"), "band", None), P(("seg", "band"), None), P())
    return jax.shard_map(
        on_device,
        mesh=mesh,
        in_specs=placed,
        out_specs=P(("seg", "chan"), None, None, "band"),
        check_vma=False,
    )
```

profile of v0, /device:TPU:0, one launch (start us, length us, event | category | flops | bytes accessed | tf_op | source)
XLA Modules:
  0.0 963.7 jit_solution(6530148631838981391)
XLA Ops:
  7.4 3.3 abs.3
  10.7 53.2 %fusion.7 = f32[128,4,3000]{0,1,2:T(4,128)} fusion(f32[128,4,3000]{0,2,1:T(8,128)S(1)} %abs.3), kind=kOutput, calls=%fused_computation.15 | output fusion | flops 196608000 | bytes 12288000 | tf_op jit(solution)/shard_map/reduce_window | solution.py:17
  63.9 20.2 %fusion.9 = f32[4,128,3000]{1,0,2:T(4,128)} fusion(f32[128,4,3000]{0,1,2:T(4,128)} %fusion.7, f32[128,4,3000]{0,2,1:T(8,128)S(1)} %copy-done.1, f32[3000]{0:T(1024)S(1)} %copy-done.2), kind=kLoop, calls=%fused_computation.17 | loop fusion | flops 4608000 | bytes 18444000 | tf_op jit(solution)/shard_map/vmap(vmap())/transpose | solution.py:28
  84.1 114.4 %while.1 = (s32[]{:T(128)}, f32[4,128,3000]{1,0,2:T(4,128)}, s32[24,3]{0,1:T(4,128)S(1)}, f32[24,128,1000]{1,2,0:T(8,128)}, s32[]{:T(128)}) while((s32[]{:T(128)}, f32[4,128,3000]{1,0,2:T(4,128)}, s32[24,3]{0,1:T(4,128)S(1)}, f32[24,128,1000]{1,2,0:T(8,128)}, s32[]{:T(128)}) %tuple.26), condition=%wide.while_cond, body=%wide.while_body.sunk | while | flops 2 | bytes 2048125 | solution.py:28
  84.8 3.3 constant_dynamic-slice_fusion.5
  88.0 0.8 constant_dynamic-update-slice_fusion.2
  89.5 3.3 constant_dynamic-slice_fusion.5
  92.8 0.8 constant_dynamic-update-slice_fusion.2
  94.3 3.3 constant_dynamic-slice_fusion.5
  97.6 0.8 constant_dynamic-update-slice_fusion.2
  99.1 3.3 constant_dynamic-slice_fusion.5
  102.3 0.8 constant_dynamic-update-slice_fusion.2
  103.8 3.3 constant_dynamic-slice_fusion.5
  107.1 0.8 constant_dynamic-update-slice_fusion.2
  108.6 3.3 constant_dynamic-slice_fusion.5
  111.9 0.8 constant_dynamic-update-slice_fusion.2
  113.4 3.3 constant_dynamic-slice_fusion.5
  116.6 0.8 constant_dynamic-update-slice_fusion.2
  118.1 3.3 constant_dynamic-slice_fusion.5
  121.4 0.8 constant_dynamic-update-slice_fusion.2
  122.9 3.3 constant_dynamic-slice_fusion.5
  126.2 0.8 constant_dynamic-update-slice_fusion.2
  127.7 3.3 constant_dynamic-slice_fusion.5
  132.4 3.3 constant_dynamic-slice_fusion.5
  135.7 0.8 constant_dynamic-update-slice_fusion.2
  137.2 3.3 constant_dynamic-slice_fusion.5
  140.5 0.8 constant_dynamic-update-slice_fusion.2
  142.0 3.3 constant_dynamic-slice_fusion.5
  145.2 0.8 constant_dynamic-update-slice_fusion.2
  146.7 3.3 constant_dynamic-slice_fusion.5
  150.0 0.8 constant_dynamic-update-slice_fusion.2
  151.5 3.3 constant_dynamic-slice_fusion.5
  154.8 0.8 constant_dynamic-update-slice_fusion.2
  156.3 3.3 constant_dynamic-slice_fusion.5
  159.5 0.8 constant_dynamic-update-slice_fusion.2
  161.0 3.3 constant_dynamic-slice_fusion.5
  164.3 0.8 constant_dynamic-update-slice_fusion.2
  165.8 3.3 constant_dynamic-slice_fusion.5
  169.1 0.8 constant_dynamic-update-slice_fusion.2
  170.6 3.3 constant_dynamic-slice_fusion.5
  175.3 3.3 constant_dynamic-slice_fusion.5
  178.6 0.8 constant_dynamic-update-slice_fusion.2
  180.1 3.3 constant_dynamic-slice_fusion.5
  183.4 0.8 constant_dynamic-update-slice_fusion.2
  184.9 3.3 constant_dynamic-slice_fusion.5
  188.1 0.8 constant_dynamic-update-slice_fusion.2
  189.6 3.3 constant_dynamic-slice_fusion.5
  192.9 0.8 constant_dynamic-update-slice_fusion.2
  194.4 3.3 constant_dynamic-slice_fusion.5
  197.7 0.8 constant_dynamic-update-slice_fusion.2
  198.5 8.1 fusion.6
  207.0 2.2 cosine_convert_fusion
  209.2 24.9 %all-gather.3.cloned.1.call-done = bf16[128,8,6,1000]{0,3,2,1:T(8,128)(2,1)} async-done(((bf16[128,4,6,1000]{0,3,2,1:T(8,128)(2,1)}), bf16[128,8,6,1000]{0,3,2,1:T(8,128)(2,1)}) %all-gather.3.cloned.1.call-update) | async-done | bytes 12288016 | tf_op jit(solution)/shard_map/all_gather | solution.py:73
  234.1 22.4 %copy.30 = bf16[128,8,6,1000]{3,2,1,0:T(8,128)(2,1)} copy(bf16[128,8,6,1000]{0,3,2,1:T(8,128)(2,1)} %all-gather.3.cloned.1.call-done) | data formatting | bytes 24576000 | tf_op jit(solution)/shard_map/all_gather | solution.py:73
  256.5 22.1 %reshape.51 = bf16[6144,1000]{1,0:T(8,128)(2,1)} reshape(bf16[128,8,6,1000]{3,2,1,0:T(8,128)(2,1)} %copy.30) | data formatting | bytes 24576000 | tf_op jit(solution)/shard_map/reshape | solution.py:46
  278.6 14.8 %multiply_reduce_fusion = (f32[6144]{0:T(1024)S(1)}, f32[6144,256]{0,1:T(8,128)}) fusion(bf16[6144,1000]{1,0:T(8,128)(2,1)} %reshape.51, bf16[1000,128]{1,0:T(8,128)(2,1)S(1)} %get-tuple-element.42, bf16[1000,128]{1,0:T(8,128)(2,1)S(1)} %get-tuple-element.41), kind=kOutput, calls=%fused_computation.12 | convolution fusion | flops 3149891584 | bytes 19116032 | tf_op jit(solution)/shard_map/dot_general | solution.py:47
  293.6 6.6 copy.31
  300.2 8.2 reshape_reshape.3
  308.5 8.4 copy.33
  316.9 5.1 multiply_convert_fusion.1
  322.1 4.0 fusion.23
  326.1 479.1 %all-gather.5.cloned.1.call-done = bf16[1024,48,2,128]{0,1,2,3:T(8,128)(2,1)} async-done(((bf16[128,48,2,128]{0,1,2,3:T(8,128)(2,1)}), bf16[1024,48,2,128]{0,1,2,3:T(8,128)(2,1)}) %all-gather.5.cloned.1.call-update) | async-done | bytes 25165840 | tf_op jit(solution)/shard_map/all_gather | solution.py:85
  805.1 34.5 %fusion = bf16[128,1024,256]{1,2,0:T(8,128)(2,1)} fusion(bf16[1024,48,2,128]{0,1,2,3:T(8,128)(2,1)} %all-gather.5.cloned.1.call-done, bf16[128,48,1,128]{0,1,2,3:T(8,128)(2,1)} %get-tuple-element.40, bf16[128,48,1,128]{0,1,2,3:T(8,128)(2,1)} %get-tuple-element.39, bf16[128,48,2,128]{0,1,2,3:T(8,128)(2,1)S(1)} %copy-done), kind=kOutput, calls=%fused_computation.4 | convolution fusion | flops 6528434176 | bytes 98566144 | tf_op jit(solution)/shard_map/iwcf,jwcf->ijf/dot_general | solution.py:62
  839.6 117.1 %copy.34 = bf16[2,128,1024,128]{3,0,2,1:T(2,128)(2,1)} copy(bf16[2,128,1024,128]{2,1,0,3:T(8,128)(2,1)} %bitcast.7) | data formatting | bytes 134217728 | tf_op jit(solution)/shard_map/convert_element_type | solution.py:65
  (72 shorter events, 18.7 us)
Async XLA Ops:
  6.5 227.6 %all-gather.3.cloned.1.call-start = ((), (), s32[]{:S(2)}) async-start(), calls=%async_computation | async-start | bytes 18432000 | tf_op jit(solution)/shard_map/all_gather | solution.py:73
  10.7 53.3 %copy-start.1 = (f32[128,4,3000]{0,2,1:T(8,128)S(1)}, f32[128,4,3000]{0,2,1:T(8,128)}, u32[]{:S(2)}) copy-start(f32[128,4,3000]{0,2,1:T(8,128)} %param.3) | copy-start | bytes 18432004
  10.7 53.3 %copy-start.2 = (f32[3000]{0:T(1024)S(1)}, f32[3000]{0:T(1024)}, u32[]{:S(2)}) copy-start(f32[3000]{0:T(1024)} %constant.15.clone.1) | copy-start | bytes 36004
  198.5 8.4 copy-start.3
  206.7 598.5 %all-gather.5.cloned.1.call-start = ((), (), s32[]{:S(2)}) async-start(), calls=%async_computation.1 | async-start | bytes 28311552 | tf_op jit(solution)/shard_map/all_gather | solution.py:85
  322.0 483.1 %copy-start = (bf16[128,48,2,128]{0,1,2,3:T(8,128)(2,1)S(1)}, bf16[128,48,2,128]{0,1,2,3:T(8,128)(2,1)}, u32[]{:S(2)}) copy-start(bf16[128,48,2,128]{0,1,2,3:T(8,128)(2,1)} %multiply_convert_fusion.1) | copy-start | bytes 9437188
Sparse Core Ops, SparseCore 0:
  206.8 27.3 all-gather.2
  322.2 482.9 all-gather.4
where the time goes:
time: 978 us; the launch traced here: 964 us
  waiting for transfers between devices  504 us (52%)
  local copies, waits for them, and re-layouts  300 us (31%)
  other arithmetic  96.9 us (10%)
  matrix products  49.3 us (5%)
  between operations  13.7 us (1%)
    all_gather x1, waiting for transfers between devices, on_device(): lax.all_gather(whitened, 'chan', axis=0, tiled=True)  479 us
    convert_element_type x1, local copies, waits for them, and re-layouts, cross_block(): (jnp.transpose(split_parts, (1, 2, 0, 3)) / win_count).astype(jnp.bfloat16)  117 us
    gather x96, local copies, waits for them, and re-layouts  114 us
    another operation x1, other arithmetic, normalize(): lax.reduce_window(magnitude, zero_val, lax.add, (1, 1, width), (1, 1, 1),...  53.2 us
    dot_general x1, matrix products, cross_block(): jnp.einsum('iwcf,jwcf->ijf', lhs_rows, other, preferred_element_type=jnp....  34.5 us
    all_gather x1, waiting for transfers between devices, on_device(): all_windows = lax.all_gather(windows, 'band', axis=1, tiled=True)  24.9 us
    all_gather x1, local copies, waits for them, and re-layouts, on_device(): all_windows = lax.all_gather(windows, 'band', axis=1, tiled=True)  22.4 us
    reshape x1, local copies, waits for them, and re-layouts, spectra(): flat_rows = windows.reshape(-1, WIN_LEN)  22.1 us
  transfers between devices with their start and end apart: 2, of which 2 were waited for; matrix products, arithmetic and copies ran while one was open for 1% of the time, Pallas kernels for 0%

commit v1 on v0

--- a/solution.py
+++ b/solution.py
@@ -1,8 +1,11 @@
+import functools
 import math
 
 import jax
 import jax.numpy as jnp
 from jax import lax
+from jax.experimental import pallas as pl
+from jax.experimental.pallas import tpu as pltpu
 from jax.sharding import PartitionSpec as P
 
 WIN_LEN = 1000
@@ -65,7 +68,7 @@
     return (jnp.transpose(split_parts, (1, 2, 0, 3)) / win_count).astype(jnp.bfloat16)
 
 
-def on_device(strain, offsets, bins):
+def on_any(strain, offsets, bins):
     normed = normalize(strain)
     windows = cut_windows(normed, offsets)
     band_count = lax.axis_size("band")
@@ -88,6 +91,218 @@
     )
 
 
+def round_up(size, step):
+    return -(-size // step) * step
+
+
+def spectra_kernel(samples, win_file, depth, offs_ref, strain_ref, hann_ref, table_ref, out_ref, mags, normed):
+    m = pl.program_id(0)
+    rows = mags.shape[0]
+    chans = mags.shape[1]
+    mags[pl.ds(0, REACH), :] = jnp.zeros((REACH, chans), jnp.float32)
+    mags[pl.ds(REACH, samples), :] = jnp.abs(strain_ref[0])
+    mags[pl.ds(REACH + samples, rows - REACH - samples), :] = jnp.zeros(
+        (rows - REACH - samples, chans), jnp.float32
+    )
+    first = mags[...]
+    total = first
+    reach = 1
+    while reach < 2 * REACH:
+        total = total + pltpu.roll(total, rows - reach, 0)
+        reach *= 2
+    total = (total + pltpu.roll(first, rows - reach, 0))[:samples]
+    pos = lax.broadcasted_iota(jnp.int32, (samples, chans), 0)
+    counts = jnp.minimum(pos + REACH, samples - 1) - jnp.maximum(pos - REACH, 0) + 1
+    normed[pl.ds(0, samples), :] = strain_ref[0] / (total / counts.astype(jnp.float32) + 1e-06)
+    spare = normed.shape[0] - samples
+    normed[pl.ds(samples, spare), :] = jnp.zeros((spare, chans), jnp.float32)
+    for k in range(win_file):
+        window = (normed[pl.ds(offs_ref[m, k], depth), :] * hann_ref[...]).astype(jnp.bfloat16)
+        spec = jnp.dot(table_ref[...], window, preferred_element_type=jnp.float32)
+        for g in range(spec.shape[0] // (2 * GROUP)):
+            part = spec[g * 2 * GROUP : (g + 1) * 2 * GROUP]
+            power = jnp.sum(part * part, axis=0, keepdims=True) / GROUP
+            out_ref[k, pl.ds(g * 2 * GROUP, 2 * GROUP), :] = (
+                part * lax.rsqrt(power + 1e-06)
+            ).astype(jnp.bfloat16)
+
+
+def own_spectra(strain, offsets, bins):
+    chans, files, samples = strain.shape
+    win_file = offsets.shape[1]
+    depth = round_up(WIN_LEN, 128)
+    table = make_table(bins)
+    parts = table.reshape(WIN_LEN, 2, bins.shape[0] // GROUP, GROUP)
+    rows = jnp.transpose(parts, (2, 1, 3, 0)).reshape(2 * bins.shape[0], WIN_LEN)
+    rows = jnp.pad(rows, ((0, 0), (0, depth - WIN_LEN)))
+    sample_pos = jnp.arange(WIN_LEN, dtype=jnp.float32)
+    taper = 0.5 - 0.5 * jnp.cos(2.0 * math.pi * (sample_pos + 0.5) / WIN_LEN)
+    taper = jnp.broadcast_to(jnp.pad(taper, (0, depth - WIN_LEN))[:, None], (depth, chans))
+    return pl.pallas_call(
+        functools.partial(spectra_kernel, samples, win_file, depth),
+        grid_spec=pltpu.PrefetchScalarGridSpec(
+            num_scalar_prefetch=1,
+            grid=(files,),
+            in_specs=[
+                pl.BlockSpec((1, samples, chans), lambda m, o: (m, 0, 0)),
+                pl.BlockSpec((depth, chans), lambda m, o: (0, 0)),
+                pl.BlockSpec((2 * bins.shape[0], depth), lambda m, o: (0, 0)),
+            ],
+            out_specs=pl.BlockSpec((win_file, 2 * bins.shape[0], chans), lambda m, o: (m, 0, 0)),
+            scratch_shapes=[
+                pltpu.VMEM((round_up(samples + 2 * REACH, 8), chans), jnp.float32),
+                pltpu.VMEM((round_up(samples - WIN_LEN + depth, 8), chans), jnp.float32),
+            ],
+        ),
+        out_shape=jax.ShapeDtypeStruct(
+            (files * win_file, 2 * bins.shape[0], chans), jnp.bfloat16
+        ),
+        compiler_params=pltpu.CompilerParams(vmem_limit_bytes=40 * 2**20),
+        name="spectra",
+    )(offsets, jnp.transpose(strain, (1, 2, 0)), taper, rows)
+
+
+FSTEP = 8
+ISTEP = 16
+
+
+def cross_kernel(win_count, slot_ref, lhs_ref, rhs_ref, place_ref, prior_ref, out_ref, low, high):
+    bins, chans, depth = lhs_ref.shape
+    half = depth // 2
+
+    @pl.when(pl.program_id(0) == 0)
+    def _():
+        @pl.loop(0, bins // FSTEP)
+        def _(step):
+            base = step * FSTEP
+            block = rhs_ref[pl.ds(base, FSTEP)]
+            turned = jnp.concatenate([-block[:, half:], block[:, :half]], axis=1)
+            both = jnp.concatenate([block, turned], axis=2).reshape(FSTEP * depth, 2 * chans)
+            mixed = jnp.dot(both, place_ref[...], preferred_element_type=jnp.float32)
+            mixed = mixed.astype(jnp.bfloat16).reshape(FSTEP, depth, 2 * chans)
+            for q in range(FSTEP):
+                prod = jnp.dot(lhs_ref[base + q], mixed[q], preferred_element_type=jnp.float32)
+                prod = prod / win_count
+                at = pl.ds(pl.multiple_of((base + q) * chans, chans), chans)
+                low[at, :] = prod[:, :chans]
+                high[at, :] = prod[:, chans:]
+
+    first = pl.program_id(0) * ISTEP
+    for q in range(ISTEP):
+        at = pl.ds(first + q, bins, stride=chans)
+        out_ref[q, pl.ds(0, chans), :] = low[at, :].T.astype(jnp.bfloat16)
+        out_ref[q, pl.ds(chans, chans), :] = high[at, :].T.astype(jnp.bfloat16)
+
+
+def cross_slot(lhs, rhs, place, prior, slot, blocks, win_count):
+    bins, chans, depth = lhs.shape
+    shape = jax.ShapeDtypeStruct((chans, 2 * chans * blocks, bins), jnp.bfloat16)
+    body = functools.partial(cross_kernel, win_count)
+    in_specs = [
+        pl.BlockSpec((bins, chans, depth), lambda i, s: (0, 0, 0)),
+        pl.BlockSpec((bins, depth, chans), lambda i, s: (0, 0, 0)),
+        pl.BlockSpec((2 * chans, 2 * chans), lambda i, s: (0, 0)),
+    ]
+    operands = [slot, lhs, rhs, place]
+    aliases = {}
+    if prior is None:
+        def body(slot_ref, lhs_ref, rhs_ref, place_ref, *rest):
+            cross_kernel(win_count, slot_ref, lhs_ref, rhs_ref, place_ref, None, *rest)
+    else:
+        in_specs.append(pl.BlockSpec(memory_space=pl.ANY))
+        operands.append(prior)
+        aliases = {4: 0}
+    return pl.pallas_call(
+        body,
+        grid_spec=pltpu.PrefetchScalarGridSpec(
+            num_scalar_prefetch=1,
+            grid=(chans // ISTEP,),
+            in_specs=in_specs,
+            out_specs=pl.BlockSpec((ISTEP, 2 * chans, bins), lambda i, s: (i, s[0], 0)),
+            scratch_shapes=[pltpu.VMEM((bins * chans, chans), jnp.float32)] * 2,
+        ),
+        out_shape=shape,
+        input_output_aliases=aliases,
+        compiler_params=pltpu.CompilerParams(vmem_limit_bytes=48 * 2**20),
+        cost_estimate=pl.CostEstimate(
+            flops=4 * bins * depth * chans * chans,
+            bytes_accessed=30 * 2**20,
+            transcendentals=0,
+        ),
+        name="cross",
+    )(*operands)
+
+
+def own_bins(strain, offsets, bins):
+    band_count = lax.axis_size("band")
+    me = lax.axis_index("band")
+    mine = own_spectra(strain, offsets, bins)
+    win_count, _, chans = mine.shape
+    mine = mine.reshape(win_count, band_count, -1, 2, GROUP, chans)
+    pieces = [lax.dynamic_index_in_dim(mine, me, 1, False)]
+    for hop in range(1, band_count):
+        sent = lax.dynamic_index_in_dim(mine, (me + hop) % band_count, 1, False)
+        pieces.append(
+            lax.ppermute(sent, "band", [(b, (b + hop) % band_count) for b in range(band_count)])
+        )
+    joined = jnp.stack(pieces)
+    turned = jnp.transpose(joined, (2, 4, 3, 0, 1, 5))
+    return turned.reshape(bins.shape[0] // band_count, 2 * band_count * win_count, chans)
+
+
+def on_line(strain, offsets, bins):
+    block = own_bins(strain, offsets, bins)
+    bin_share, depth, chans = block.shape
+    lhs = jnp.transpose(block, (0, 2, 1))
+    spot = jnp.arange(2 * chans)
+    place = (spot[None, :] == (2 * (spot % chans) + spot // chans)[:, None]).astype(jnp.bfloat16)
+    me = lax.axis_index("chan")
+    z, x = me // 2, me % 2
+
+    def along(value, step, reach):
+        ends = [(a, a + step) for a in range(4) if 0 <= a + step < 4 and 0 <= a - (reach - 1) * step < 4]
+        return lax.ppermute(value, "chan", [(2 * a + s, 2 * b + s) for a, b in ends for s in range(2)])
+
+    def across(value):
+        return lax.ppermute(value, "chan", [(c, c ^ 1) for c in range(8)])
+
+    def cross(value, number, prior):
+        return cross_slot(lhs, value, place, prior, number.astype(jnp.int32).reshape(1), 8, depth // 2)
+
+    near_z = jnp.where(z > 0, z - 1, z + 1)
+    mid_z = jnp.where(z >= 2, z - 2, z + 2)
+    last_z = jnp.where(z == 0, 3, jnp.where(z == 3, 0, z + 1))
+
+    up1, down1, other = along(block, 1, 1), along(block, -1, 1), across(block)
+    out = cross(block, me, None)
+    up1, down1, out = lax.optimization_barrier((up1, down1, out))
+
+    near = jnp.where(z > 0, up1, down1)
+    up2, down2, near_other = along(up1, 1, 2), along(down1, -1, 2), across(near)
+    out = cross(other, 2 * z + 1 - x, out)
+    out = cross(near, 2 * near_z + x, out)
+    up2, down2, out = lax.optimization_barrier((up2, down2, out))
+
+    mid = jnp.where(z >= 2, up2, down2)
+    up3, down3, mid_other = along(mid, 1, 3), along(mid, -1, 3), across(mid)
+    out = cross(near_other, 2 * near_z + 1 - x, out)
+    out = cross(mid, 2 * mid_z + x, out)
+    up3, down3, out = lax.optimization_barrier((up3, down3, out))
+
+    last = jnp.where(z == 0, down3, jnp.where(z == 3, up3, down1))
+    last_other = across(last)
+    out = cross(mid_other, 2 * mid_z + 1 - x, out)
+    out = cross(last, 2 * last_z + x, out)
+    out = cross(last_other, 2 * last_z + 1 - x, out)
+    return out.reshape(chans, 8 * chans, 2, bin_share)
+
+
+def on_device(strain, offsets, bins):
+    if strain.shape[0] == 128 and lax.axis_size("chan") == 8 and bins.shape[0] // lax.axis_size("band") == 128:
+        return on_line(strain, offsets, bins)
+    return on_any(strain, offsets, bins)
+
+
 def solution(mesh):
     placed = (P(("seg", "chan"), "band", None), P(("seg", "band"), None), P())
     return jax.shard_map(

time: 978 us -> 354 us (0.36); the launches traced: 964 us -> 354 us
  waiting for transfers between devices: 504 us -> 108 us
  local copies, waits for them, and re-layouts: 300 us -> 10.2 us
  Pallas kernels: 0 us -> 195 us
  other arithmetic: 96.9 us -> 17.6 us
  matrix products: 49.3 us -> 0 us
  starting transfers between devices: 0.22 us -> 21.8 us
  between operations: 13.7 us -> 0.21 us
    all_gather x2 -> x0, waiting for transfers between devices: 504 us -> none  [the longest x1 479 us: on_device(): lax.all_gather(whitened, 'chan', axis=0, tiled=True)]
    pallas_call x0 -> x9, Pallas kernels: none -> 195 us  [the longest x8 178 us: cross_slot(): pl.pallas_call(body, grid_spec=pltpu.PrefetchScalarGridSpec(num_scalar_pr...]
    convert_element_type x1 -> x0, local copies, waits for them, and re-layouts: 117 us -> none  [cross_block(): (jnp.transpose(split_parts, (1, 2, 0, 3)) / win_count).astype(jnp.bfloat16)]
    gather x97 -> x0, local copies, waits for them, and re-layouts: 114 us -> none
    ppermute x0 -> x11, waiting for transfers between devices: none -> 108 us  [the longest x6 85.4 us: along(): lax.ppermute(value, 'chan', [(2 * a + s, 2 * b + s) for a, b in ends for...]
    another operation x2, other arithmetic: 55.4 us -> 6.05 us  [the longest x1 53.2 us: normalize(): lax.reduce_window(magnitude, zero_val, lax.add, (1, 1, width), (1, 1, 1),...]
    dot_general x2 -> x0, matrix products: 49.3 us -> none  [the longest x1 34.5 us: cross_block(): jnp.einsum('iwcf,jwcf->ijf', lhs_rows, other, preferred_element_type=jnp....]
    all_gather x1 -> x0, local copies, waits for them, and re-layouts: 22.4 us -> none  [on_device(): all_windows = lax.all_gather(windows, 'band', axis=1, tiled=True)]
  transfers between devices with their start and end apart: 2 -> 11, of which waited for: 2 -> 6; matrix products, arithmetic and copies ran while one was open for 1% -> 5% of each run, Pallas kernels for 0% -> 44%
where the time goes in v1:
time: 354 us
  Pallas kernels  195 us (55%)
  waiting for transfers between devices  108 us (31%)
  starting transfers between devices  21.8 us (6%)
  other arithmetic  17.6 us (5%)
  local copies, waits for them, and re-layouts  10.2 us (3%)
    pallas_call x8, Pallas kernels, cross_slot(): pl.pallas_call(body, grid_spec=pltpu.PrefetchScalarGridSpec(num_scalar_pr...  178 us
    ppermute x6, waiting for transfers between devices, along(): lax.ppermute(value, 'chan', [(2 * a + s, 2 * b + s) for a, b in ends for...  85.4 us
    ppermute x4, waiting for transfers between devices, across(): return lax.ppermute(value, 'chan', [(c, c ^ 1) for c in range(8)])  20.9 us
    pallas_call x1, Pallas kernels, own_spectra(): pl.pallas_call(functools.partial(spectra_kernel, samples, win_file, depth...  17.2 us
    ppermute x6, starting transfers between devices, along(): lax.ppermute(value, 'chan', [(2 * a + s, 2 * b + s) for a, b in ends for...  15.2 us
  transfers between devices with their start and end apart: 11, of which 6 were waited for; matrix products, arithmetic and copies ran while one was open for 5% of the time, Pallas kernels for 44%

profile of v1, /device:TPU:0, one launch (start us, length us, event | category | flops | bytes accessed | tf_op | source)
XLA Modules:
  0.0 353.6 jit_solution(891459697106687707)
XLA Ops:
  0.0 0.0 copy-start.1
  0.1 5.8 %cosine_convert_fusion = (bf16[1000,1,2,128]{0,3,1,2:T(8,128)(2,1)S(1)}, bf16[1000,1,2,128]{0,3,1,2:T(8,128)(2,1)S(1)}) fusion(s32[2,128]{1,0:T(2,128)} %bitcast.38), kind=kLoop, calls=%fused_computation.11 | loop fusion | flops 3072000 | bytes 1025024 | tf_op jit(solution)/shard_map/convert
  5.8 0.1 pad_maximum_fusion.1
  6.0 0.1 pad.9.table_ref
  6.1 0.2 broadcast_in_dim.2.hann_ref
  6.3 0.0 copy-done.1
  6.3 0.0 copy-start
  6.3 2.7 copy-done
  9.0 17.2 %spectra.1 = bf16[24,512,128]{2,1,0:T(8,128)(2,1)S(1)} custom-call(s32[4,6]{1,0:T(4,128)S(1)} %copy-done.1, f32[4,3000,128]{2,1,0:T(8,128)S(1)} %bitcast.33, f32[1024,128]{1,0:T(8,128)S(1)} %broadcast_in_dim.2.hann_ref, bf16[512,1024]{1,0:T(8,128)(2,1)S(1)} %pad.9.table_ref), custom_call_target="tpu_custom_call" | custom-call | tf_op jit(solution)/shard_map/spectra/pallas_call | solution.py:141
  26.3 0.2 constant_dynamic-slice_fusion.1
  26.5 1.0 copy.23
  27.5 0.5 collective-permute-start
  28.1 1.0 copy.24
  29.1 2.0 collective-permute-done
  31.1 0.3 pad_maximum_fusion
  31.4 6.6 %collective-permute-start.1 = (bf16[128,96,128]{2,1,0:T(8,128)(2,1)S(1)}, bf16[128,96,128]{2,1,0:T(8,128)(2,1)}, u32[]{:S(2)}, u32[]{:S(2)}) collective-permute-start(bf16[128,96,128]{2,1,0:T(8,128)(2,1)S(1)} %bitcast.27), channel_id=1, source_target_pairs={{0,4},{2,6},{4,8},{6,10},{8,12},{10,14},{1,5},{3,7},{5,9},{7,11},{... | collective-permute-start | bytes 9437192 | tf_op jit(solution)/shard_map/ppermute | solution.py:264
  37.9 1.3 collective-permute-start.2
  39.2 1.6 collective-permute-start.5
  40.8 0.1 fusion.5.place_ref
  40.9 4.9 %copy.20.lhs_ref = bf16[128,128,96]{2,1,0:T(8,128)(2,1)} copy(bf16[128,128,96]{1,2,0:T(8,128)(2,1)S(1)} %bitcast.30) | data formatting | bytes 6291456 | tf_op jit(solution)/shard_map/transpose | solution.py:256
  45.8 21.5 %cross.8.prior_ref = bf16[128,2048,128]{2,1,0:T(8,128)(2,1)} custom-call(s32[1]{0:T(128)} %bitcast.13.slot_ref, bf16[128,128,96]{2,1,0:T(8,128)(2,1)} %copy.20.lhs_ref, bf16[128,96,128]{2,1,0:T(8,128)(2,1)S(1)} %bitcast.31, bf16[256,256]{1,0:T(8,128)(2,1)S(1)} %fusion.5.place_ref), custom_call_target="tpu_custom_call" | custom-call | flops 805306368 | bytes 31457280 | tf_op jit(solution)/shard_map/cross/pallas_call | solution.py:215
  67.3 36.5 %collective-permute-done.1 = bf16[128,96,128]{2,1,0:T(8,128)(2,1)} collective-permute-done((bf16[128,96,128]{2,1,0:T(8,128)(2,1)S(1)}, bf16[128,96,128]{2,1,0:T(8,128)(2,1)}, u32[]{:S(2)}, u32[]{:S(2)}) %collective-permute-start.1) | collective-permute-done | bytes 3145760 | tf_op jit(solution)/shard_map/ppermute | solution.py:264
  103.9 5.9 %collective-permute-done.2 = bf16[128,96,128]{2,1,0:T(8,128)(2,1)} collective-permute-done((bf16[128,96,128]{2,1,0:T(8,128)(2,1)S(1)}, bf16[128,96,128]{2,1,0:T(8,128)(2,1)}, u32[]{:S(2)}, u32[]{:S(2)}) %collective-permute-start.2) | collective-permute-done | bytes 3145760 | tf_op jit(solution)/shard_map/ppermute | solution.py:264
  109.8 2.3 collective-permute-start.3
  112.1 1.5 collective-permute-start.4
  113.6 4.0 %broadcast_select_fusion.rhs_ref = bf16[128,96,128]{2,1,0:T(8,128)(2,1)} fusion(bf16[128,96,128]{2,1,0:T(8,128)(2,1)} %collective-permute-done.1, bf16[128,96,128]{2,1,0:T(8,128)(2,1)} %collective-permute-done.2, pred[]{:T(512)S(6)} %gt.4), kind=kLoop, calls=%fused_computation.2 | loop fusion | flops 1572864 | bytes 9437185 | tf_op jit(solution)/shard_map/jit(_where)/select_n | solution.py:280
  117.6 1.5 collective-permute-start.8
  119.1 0.0 collective-permute-done.5.rhs_ref
  119.1 22.5 %cross.9.prior_ref = bf16[128,2048,128]{2,1,0:T(8,128)(2,1)} custom-call(s32[1]{0:T(128)} %bitcast.15.slot_ref, bf16[128,128,96]{2,1,0:T(8,128)(2,1)} %copy.20.lhs_ref, bf16[128,96,128]{2,1,0:T(8,128)(2,1)} %collective-permute-done.5.rhs_ref, bf16[256,256]{1,0:T(8,128)(2,1)S(1)} %fusion.5.place_ref, ...), custom_call_target="tpu_custom_call", output_to_operand_aliasing={{}: (4, {})} | custom-call | flops 805306368 | bytes 31457280 | tf_op jit(solution)/shard_map/cross/pallas_call | solution.py:215
  141.6 22.5 %cross.10.prior_ref = bf16[128,2048,128]{2,1,0:T(8,128)(2,1)} custom-call(s32[1]{0:T(128)} %bitcast.14.slot_ref, bf16[128,128,96]{2,1,0:T(8,128)(2,1)} %copy.20.lhs_ref, bf16[128,96,128]{2,1,0:T(8,128)(2,1)} %broadcast_select_fusion.rhs_ref, bf16[256,256]{1,0:T(8,128)(2,1)S(1)} %fusion.5.place_ref, ...), custom_call_target="tpu_custom_call", output_to_operand_aliasing={{}: (4, {})} | custom-call | flops 805306368 | bytes 31457280 | tf_op jit(solution)/shard_map/cross/pallas_call | solution.py:215
  164.1 0.0 collective-permute-done.3
  164.2 19.8 %collective-permute-done.4 = bf16[128,96,128]{2,1,0:T(8,128)(2,1)} collective-permute-done((bf16[128,96,128]{2,1,0:T(8,128)(2,1)}, bf16[128,96,128]{2,1,0:T(8,128)(2,1)}, u32[]{:S(2)}, u32[]{:S(2)}) %collective-permute-start.4) | collective-permute-done | bytes 3145760 | tf_op jit(solution)/shard_map/ppermute | solution.py:264
  184.0 2.2 broadcast_select_fusion.1.rhs_ref
  186.2 2.3 collective-permute-start.6
  188.5 1.3 collective-permute-start.7
  189.8 1.6 collective-permute-start.10
  191.4 0.0 collective-permute-done.8.rhs_ref
  191.4 22.5 %cross.11.prior_ref = bf16[128,2048,128]{2,1,0:T(8,128)(2,1)} custom-call(s32[1]{0:T(128)} %bitcast.17.slot_ref, bf16[128,128,96]{2,1,0:T(8,128)(2,1)} %copy.20.lhs_ref, bf16[128,96,128]{2,1,0:T(8,128)(2,1)} %collective-permute-done.8.rhs_ref, bf16[256,256]{1,0:T(8,128)(2,1)S(1)} %fusion.5.place_ref, ...), custom_call_target="tpu_custom_call", output_to_operand_aliasing={{}: (4, {})} | custom-call | flops 805306368 | bytes 31457280 | tf_op jit(solution)/shard_map/cross/pallas_call | solution.py:215
  213.9 21.5 %cross.12.prior_ref = bf16[128,2048,128]{2,1,0:T(8,128)(2,1)} custom-call(s32[1]{0:T(128)} %bitcast.16.slot_ref, bf16[128,128,96]{2,1,0:T(8,128)(2,1)} %copy.20.lhs_ref, bf16[128,96,128]{2,1,0:T(8,128)(2,1)S(1)} %broadcast_select_fusion.1.rhs_ref, bf16[256,256]{1,0:T(8,128)(2,1)S(1)} %fusion.5.place_ref, ...), custom_call_target="tpu_custom_call", output_to_operand_aliasing={{}: (4, {})} | custom-call | flops 805306368 | bytes 31457280 | tf_op jit(solution)/shard_map/cross/pallas_call | solution.py:215
  235.4 0.0 collective-permute-done.6
  235.4 23.1 %collective-permute-done.7 = bf16[128,96,128]{2,1,0:T(8,128)(2,1)} collective-permute-done((bf16[128,96,128]{2,1,0:T(8,128)(2,1)S(1)}, bf16[128,96,128]{2,1,0:T(8,128)(2,1)}, u32[]{:S(2)}, u32[]{:S(2)}) %collective-permute-start.7) | collective-permute-done | bytes 3145760 | tf_op jit(solution)/shard_map/ppermute | solution.py:264
  258.6 5.0 %select_select_fusion.rhs_ref = bf16[128,96,128]{2,1,0:T(8,128)(2,1)} fusion(bf16[128,96,128]{2,1,0:T(8,128)(2,1)} %collective-permute-done.7, bf16[128,96,128]{2,1,0:T(8,128)(2,1)} %collective-permute-done.6, bf16[128,96,128]{2,1,0:T(8,128)(2,1)} %collective-permute-done.2, pred[]{:T(512)S(6)} %eq.71, pred[]{:T(512)S(6)} %eq.70), kind=kLoop, calls=%fused_computation.1 | loop fusion | flops 3145728 | bytes 12582914 | tf_op jit(solution)/shard_map/jit(_where)/select_n | solution.py:292
  263.6 1.5 collective-permute-start.9
  265.1 0.0 collective-permute-done.10.rhs_ref
  265.1 22.5 %cross.13.prior_ref = bf16[128,2048,128]{2,1,0:T(8,128)(2,1)} custom-call(s32[1]{0:T(128)} %bitcast.19.slot_ref, bf16[128,128,96]{2,1,0:T(8,128)(2,1)} %copy.20.lhs_ref, bf16[128,96,128]{2,1,0:T(8,128)(2,1)} %collective-permute-done.10.rhs_ref, bf16[256,256]{1,0:T(8,128)(2,1)S(1)} %fusion.5.place_ref, ...), custom_call_target="tpu_custom_call", output_to_operand_aliasing={{}: (4, {})} | custom-call | flops 805306368 | bytes 31457280 | tf_op jit(solution)/shard_map/cross/pallas_call | solution.py:215
  287.6 22.5 %cross.14.prior_ref = bf16[128,2048,128]{2,1,0:T(8,128)(2,1)} custom-call(s32[1]{0:T(128)} %bitcast.18.slot_ref, bf16[128,128,96]{2,1,0:T(8,128)(2,1)} %copy.20.lhs_ref, bf16[128,96,128]{2,1,0:T(8,128)(2,1)} %select_select_fusion.rhs_ref, bf16[256,256]{1,0:T(8,128)(2,1)S(1)} %fusion.5.place_ref, ...), custom_call_target="tpu_custom_call", output_to_operand_aliasing={{}: (4, {})} | custom-call | flops 805306368 | bytes 31457280 | tf_op jit(solution)/shard_map/cross/pallas_call | solution.py:215
  310.2 20.9 %collective-permute-done.9.rhs_ref = bf16[128,96,128]{2,1,0:T(8,128)(2,1)} collective-permute-done((bf16[128,96,128]{2,1,0:T(8,128)(2,1)}, bf16[128,96,128]{2,1,0:T(8,128)(2,1)}, u32[]{:S(2)}, u32[]{:S(2)}) %collective-permute-start.9) | collective-permute-done | bytes 3145760 | tf_op jit(solution)/shard_map/ppermute | solution.py:267
  331.1 22.5 %cross.15 = bf16[128,2048,128]{2,1,0:T(8,128)(2,1)} custom-call(s32[1]{0:T(128)} %bitcast.slot_ref, bf16[128,128,96]{2,1,0:T(8,128)(2,1)} %copy.20.lhs_ref, bf16[128,96,128]{2,1,0:T(8,128)(2,1)} %collective-permute-done.9.rhs_ref, bf16[256,256]{1,0:T(8,128)(2,1)S(1)} %fusion.5.place_ref, ...), custom_call_target="tpu_custom_call", output_to_operand_aliasing={{}: (4, {})} | custom-call | flops 805306368 | bytes 31457280 | tf_op jit(solution)/shard_map/cross/pallas_call | solution.py:215
  (3 shorter events, 0.1 us)
Async XLA Ops:
  0.0 6.3 %copy-start.1 = (s32[4,6]{1,0:T(4,128)S(1)}, s32[4,6]{1,0:T(4,128)}, u32[]{:S(2)}) copy-start(s32[4,6]{1,0:T(4,128)} %offs_ref.1) | copy-start | bytes 292
  6.3 2.7 copy-start
  27.5 3.5 %collective-permute-start = (bf16[24,1,2,128,128]{4,0,2,3,1:T(8,128)(2,1)S(1)}, bf16[24,1,2,128,128]{4,0,2,3,1:T(8,128)(2,1)S(1)}, u32[]{:S(2)}, u32[]{:S(2)}) collective-permute-start(bf16[24,1,2,128,128]{4,0,2,3,1:T(8,128)(2,1)S(1)} %bitcast.36), channel_id=1, source_target_pairs={{0,1},{1,0},{2,3},{3,2},{4,5},{5,4},{6,7},{7,6},{8,9},{9,8},{10,11... | collective-permute-start | bytes 4718600 | tf_op jit(solution)/shard_map/ppermute | solution.py:246
  31.4 72.5 %collective-permute-start.1 = (bf16[128,96,128]{2,1,0:T(8,128)(2,1)S(1)}, bf16[128,96,128]{2,1,0:T(8,128)(2,1)}, u32[]{:S(2)}, u32[]{:S(2)}) collective-permute-start(bf16[128,96,128]{2,1,0:T(8,128)(2,1)S(1)} %bitcast.27), channel_id=1, source_target_pairs={{0,4},{2,6},{4,8},{6,10},{8,12},{10,14},{1,5},{3,7},{5,9},{7,11},{... | collective-permute-start | bytes 9437192 | tf_op jit(solution)/shard_map/ppermute | solution.py:264
  37.9 71.8 %collective-permute-start.2 = (bf16[128,96,128]{2,1,0:T(8,128)(2,1)S(1)}, bf16[128,96,128]{2,1,0:T(8,128)(2,1)}, u32[]{:S(2)}, u32[]{:S(2)}) collective-permute-start(bf16[128,96,128]{2,1,0:T(8,128)(2,1)S(1)} %bitcast.28), channel_id=1, source_target_pairs={{4,0},{6,2},{8,4},{10,6},{12,8},{14,10},{5,1},{7,3},{9,5},{11,7},{... | collective-permute-start | bytes 9437192 | tf_op jit(solution)/shard_map/ppermute | solution.py:264
  39.2 79.9 %collective-permute-start.5 = (bf16[128,96,128]{2,1,0:T(8,128)(2,1)S(1)}, bf16[128,96,128]{2,1,0:T(8,128)(2,1)}, u32[]{:S(2)}, u32[]{:S(2)}) collective-permute-start(bf16[128,96,128]{2,1,0:T(8,128)(2,1)S(1)} %bitcast.29), channel_id=1, source_target_pairs={{0,2},{2,0},{4,6},{6,4},{8,10},{10,8},{12,14},{14,12},{1,3},{3,1},... | collective-permute-start | bytes 9437192 | tf_op jit(solution)/shard_map/ppermute | solution.py:267
  109.8 54.4 %collective-permute-start.3 = (bf16[128,96,128]{2,1,0:T(8,128)(2,1)}, bf16[128,96,128]{2,1,0:T(8,128)(2,1)}, u32[]{:S(2)}, u32[]{:S(2)}) collective-permute-start(bf16[128,96,128]{2,1,0:T(8,128)(2,1)} %collective-permute-done.1), channel_id=1, source_target_pairs={{4,8},{6,10},{8,12},{10,14},{5,9},{7,11},{9,13},{11,15},{20,24},{2... | collective-permute-start | bytes 9437192 | tf_op jit(solution)/shard_map/ppermute | solution.py:264
  112.1 71.9 %collective-permute-start.4 = (bf16[128,96,128]{2,1,0:T(8,128)(2,1)}, bf16[128,96,128]{2,1,0:T(8,128)(2,1)}, u32[]{:S(2)}, u32[]{:S(2)}) collective-permute-start(bf16[128,96,128]{2,1,0:T(8,128)(2,1)} %collective-permute-done.2), channel_id=1, source_target_pairs={{4,0},{6,2},{8,4},{10,6},{5,1},{7,3},{9,5},{11,7},{20,16},{22,18},... | collective-permute-start | bytes 9437192 | tf_op jit(solution)/shard_map/ppermute | solution.py:264
  117.6 73.8 %collective-permute-start.8 = (bf16[128,96,128]{2,1,0:T(8,128)(2,1)}, bf16[128,96,128]{2,1,0:T(8,128)(2,1)}, u32[]{:S(2)}, u32[]{:S(2)}) collective-permute-start(bf16[128,96,128]{2,1,0:T(8,128)(2,1)} %broadcast_select_fusion.rhs_ref), channel_id=1, source_target_pairs={{0,2},{2,0},{4,6},{6,4},{8,10},{10,8},{12,14},{14,12},{1,3},{3,1},... | collective-permute-start | bytes 9437192 | tf_op jit(solution)/shard_map/ppermute | solution.py:267
  186.2 49.3 %collective-permute-start.6 = (bf16[128,96,128]{2,1,0:T(8,128)(2,1)S(1)}, bf16[128,96,128]{2,1,0:T(8,128)(2,1)}, u32[]{:S(2)}, u32[]{:S(2)}) collective-permute-start(bf16[128,96,128]{2,1,0:T(8,128)(2,1)S(1)} %broadcast_select_fusion.1.rhs_ref), channel_id=1, source_target_pairs={{8,12},{10,14},{9,13},{11,15},{24,28},{26,30},{25,29},{27,31}} | collective-permute-start | bytes 9437192 | tf_op jit(solution)/shard_map/ppermute | solution.py:264
  188.5 70.1 %collective-permute-start.7 = (bf16[128,96,128]{2,1,0:T(8,128)(2,1)S(1)}, bf16[128,96,128]{2,1,0:T(8,128)(2,1)}, u32[]{:S(2)}, u32[]{:S(2)}) collective-permute-start(bf16[128,96,128]{2,1,0:T(8,128)(2,1)S(1)} %broadcast_select_fusion.1.rhs_ref), channel_id=1, source_target_pairs={{4,0},{6,2},{5,1},{7,3},{20,16},{22,18},{21,17},{23,19}} | collective-permute-start | bytes 9437192 | tf_op jit(solution)/shard_map/ppermute | solution.py:264
  189.8 75.3 %collective-permute-start.10 = (bf16[128,96,128]{2,1,0:T(8,128)(2,1)S(1)}, bf16[128,96,128]{2,1,0:T(8,128)(2,1)}, u32[]{:S(2)}, u32[]{:S(2)}) collective-permute-start(bf16[128,96,128]{2,1,0:T(8,128)(2,1)S(1)} %broadcast_select_fusion.1.rhs_ref), channel_id=1, source_target_pairs={{0,2},{2,0},{4,6},{6,4},{8,10},{10,8},{12,14},{14,12},{1,3},{3,1},... | collective-permute-start | bytes 9437192 | tf_op jit(solution)/shard_map/ppermute | solution.py:267
  263.6 67.5 %collective-permute-start.9 = (bf16[128,96,128]{2,1,0:T(8,128)(2,1)}, bf16[128,96,128]{2,1,0:T(8,128)(2,1)}, u32[]{:S(2)}, u32[]{:S(2)}) collective-permute-start(bf16[128,96,128]{2,1,0:T(8,128)(2,1)} %select_select_fusion.rhs_ref), channel_id=1, source_target_pairs={{0,2},{2,0},{4,6},{6,4},{8,10},{10,8},{12,14},{14,12},{1,3},{3,1},... | collective-permute-start | bytes 9437192 | tf_op jit(solution)/shard_map/ppermute | solution.py:267
